TPU v7x, 32 devices: a whole 2x2x4 slice. The times are simulated.
32 devices in a mesh: grid: 4 (over z), basis: 8 (over y, x, core).
Axes of the slice: x: 2, y: 2, z: 4, core: 2. Of those that a mesh axis runs over, the one named last changes fastest.
Arguments:
- basis_values: bfloat16 [512, 256, 512], P(('grid', 'basis')), may hold values from -6 to 6
- weights: float32 [512, 256], P(('grid', 'basis')), may hold values from 0.1 to 1
- points: bfloat16 [512, 3, 256], P(('grid', 'basis')), may hold values from 0 to 1
- block_lists: int32 [512, 4], P(('grid', 'basis')), may hold values from 0 to 31, as said below
- counts: int32 [8, 4], P('basis', 'grid'), may hold values from 1 to 16, 32 in all within a row
- density: bfloat16 [4096, 4096], P('basis'), may hold values from -0.25 to 0.25
- centers: float32 [3, 4096], replicated, may hold values from 0 to 1
- block_centers: float32 [3, 32], replicated, may hold values from 0 to 1
- block_exponents: float32 [32], replicated, may hold values from 2 to 20
Outputs:
- exchange_matrix: float32 [4096, 4096], P('basis', 'grid')
Inputs may be any that keep to these rules, and one draw needn't show every extreme that they name: `block_lists`: each row names 4 different blocks. The rows of all devices with the same basis index name together exactly 8 different blocks, consecutive ones counted on from 31 to 0, and the rows of each such device name all 8 of them; one of them is named by every row of those devices. The blocks of basis index 0 begin at block 31. Entry [b, g] counts the live batches of the device at grid index g and basis index b, which are its first ones. Each row sums to 32 and its largest entry is 16.
All inputs are finite; a program needn't handle non-finite values.
Results may differ from a plain program's by a relative error of at most 0.0018.
Values may be sent and summed in bfloat16 or wider, within the bound.
A program may use at most 128 MiB of HBM per device.

v0:
```python
import math

import jax
import jax.numpy as jnp
from jax import lax
from jax.sharding import PartitionSpec as P

TB = 128
LB = 4
CL = 8
P_SIZE = 256


def boys_table(points_f, blocks, block_centers, block_exponents):
    centre = block_centers[:, blocks]
    middle = 0.5 * (centre[:, :, :, None] + centre[:, :, None, :])
    exponents = block_exponents[blocks]
    rate_pair = 0.5 * (exponents[:, :, None] + exponents[:, None, :])
    offset = points_f.transpose(1, 0, 2)[:, :, None, None, :] - middle[:, :, :, :, None]
    distance = jnp.sum(offset * offset, axis=0)
    tau_value = rate_pair[:, :, :, None] * distance + 0.05
    root_value = jnp.sqrt(tau_value)
    return 0.5 * math.sqrt(math.pi) * lax.erf(root_value) / root_value


def cluster_of(block_lists, block_count):
    present = jnp.any(
        block_lists.reshape(-1)[:, None] == jnp.arange(block_count, dtype=jnp.int32)[None, :],
        axis=0,
    )
    ranked = jnp.cumsum(present.astype(jnp.int32)) - 1
    target = jnp.where(present, ranked, CL)
    return (
        jnp.zeros((CL,), jnp.int32)
        .at[target]
        .set(jnp.arange(block_count, dtype=jnp.int32), mode="drop")
    )


def places_in(lists, cluster):
    matched = lists[:, :, None] == cluster[None, None, :]
    return jnp.sum(jnp.where(matched, jnp.arange(CL, dtype=jnp.int32)[None, None, :], 0), axis=2)


def cluster_coupling(cluster, centers):
    functions = (cluster[:, None] * TB + jnp.arange(TB, dtype=jnp.int32)[None, :]).reshape(CL * TB)
    where_at = centers[:, functions]
    spread = where_at[:, :, None] - where_at[:, None, :]
    distance = jnp.sum(spread * spread, axis=0)
    sharpness = float(centers.shape[1]) ** (2.0 / 3.0)
    return jnp.exp(-sharpness * distance).astype(jnp.bfloat16).reshape(CL, TB, CL, TB)


def potential_rows(mapped, points, lists, places, coupled_all, block_centers, block_exponents):
    batch_total = mapped.shape[0]
    group_size = math.gcd(batch_total, 4)

    def one_group(pieces):
        mapped_part, points_part, lists_part, places_part = pieces
        coupled = coupled_all[places_part[:, :, None], :, places_part[:, None, :], :]
        factor = boys_table(
            points_part.astype(jnp.float32), lists_part, block_centers, block_exponents
        )
        partial_rows = jnp.einsum(
            "kpuj,ktuij->kptui", mapped_part, coupled, preferred_element_type=jnp.float32
        )
        boys_weight = factor.transpose(0, 3, 1, 2)[:, :, :, :, None]
        return jnp.sum(partial_rows * boys_weight, axis=3).astype(jnp.bfloat16)

    shaped = tuple(
        (
            member.reshape((batch_total // group_size, group_size) + member.shape[1:])
            for member in (mapped, points, lists, places)
        )
    )
    result = lax.map(one_group, shaped)
    return result.reshape((batch_total,) + result.shape[2:])


def body(
    basis_values,
    weights,
    points,
    block_lists,
    counts,
    density,
    centers,
    block_centers,
    block_exponents,
):
    basis_size = lax.axis_size("basis")
    grid_size = lax.axis_size("grid")
    block_count = block_exponents.shape[0]
    owned_blocks = block_count // basis_size
    per_owner = min(owned_blocks, CL)
    batches = basis_values.shape[0]
    slot_total = basis_size * per_owner
    cluster = cluster_of(block_lists, block_count)
    places = places_in(block_lists, cluster)
    owner_of = cluster // owned_blocks
    lower = jnp.arange(CL, dtype=jnp.int32)[None, :] < jnp.arange(CL, dtype=jnp.int32)[:, None]
    before = jnp.sum(((owner_of[None, :] == owner_of[:, None]) & lower).astype(jnp.int32), axis=1)
    slot_of = owner_of * per_owner + before
    row_ask = (
        jnp.full((slot_total,), owned_blocks, jnp.int32).at[slot_of].set(cluster % owned_blocks)
    )
    column_ask = jnp.broadcast_to(cluster[None, :], (slot_total, CL))
    density_tiles = density.reshape(owned_blocks, TB, block_count, TB).transpose(0, 2, 1, 3)
    column_part = CL
    columns_in = lax.all_to_all(
        column_ask.reshape(basis_size, per_owner, CL),
        "basis",
        split_axis=0,
        concat_axis=0,
        tiled=True,
    )
    rows_in = lax.all_to_all(
        row_ask.reshape(basis_size, per_owner), "basis", split_axis=0, concat_axis=0, tiled=True
    )
    safe_rows = jnp.minimum(rows_in, owned_blocks - 1)
    tile_rows = density_tiles[safe_rows[:, :, None], columns_in]
    returned = lax.all_to_all(tile_rows, "basis", split_axis=0, concat_axis=0, tiled=True)
    own_tiles = returned.reshape(slot_total, column_part, TB, TB)[slot_of]
    dens_list = own_tiles[places[:, :, None], places[:, None, :]]
    mapped = jnp.einsum(
        "ktuij,kpuj->kpti",
        dens_list,
        basis_values.reshape(batches, P_SIZE, LB, TB),
        preferred_element_type=jnp.float32,
    ).astype(jnp.bfloat16)
    coupled_all = cluster_coupling(cluster, centers)
    position = jnp.arange(batches, dtype=jnp.int32)
    live_count = counts[0, 0]
    is_live = position < live_count
    potential = potential_rows(
        mapped, points, block_lists, places, coupled_all, block_centers, block_exponents
    )
    scaled = jnp.where(is_live[:, None], weights, 0.0) / P_SIZE
    weighted = (basis_values * scaled[:, :, None]).astype(jnp.bfloat16)
    seg_width = CL * TB // grid_size
    picked = (places[:, :, None] == jnp.arange(CL, dtype=jnp.int32)[None, None, :]).astype(
        jnp.bfloat16
    )
    spread_rows = (
        jnp.einsum(
            "ktc,kpti->kpci",
            picked,
            weighted.reshape(batches, P_SIZE, LB, TB),
            preferred_element_type=jnp.float32,
        )
        .astype(jnp.bfloat16)
        .reshape(batches * P_SIZE, CL * TB)
    )
    spread_cols = (
        jnp.einsum("ktc,kpti->kpci", picked, potential, preferred_element_type=jnp.float32)
        .astype(jnp.bfloat16)
        .reshape(batches * P_SIZE, CL * TB)
    )
    segment = lax.psum_scatter(
        jnp.einsum("ka,kb->ab", spread_cols, spread_rows, preferred_element_type=jnp.float32),
        "grid",
        scatter_dimension=0,
        tiled=True,
    )
    outgoing = (
        jnp.zeros((slot_total, seg_width, TB), jnp.float32)
        .at[slot_of]
        .set(segment.reshape(seg_width, CL, TB).transpose(1, 0, 2))
    )
    incoming = lax.all_to_all(
        outgoing.reshape(basis_size, per_owner, seg_width, TB),
        "basis",
        split_axis=0,
        concat_axis=0,
        tiled=True,
    )
    offset = lax.axis_index("grid") * seg_width + jnp.arange(seg_width, dtype=jnp.int32)
    column_fn = columns_in[:, 0, :][:, offset // TB] * TB + (offset % TB)[None, :]
    gathered_at = (
        jnp.zeros((owned_blocks, block_count * TB, TB), jnp.float32)
        .at[rows_in[:, :, None], column_fn[:, None, :]]
        .add(incoming, mode="drop")
    )
    summed = lax.psum_scatter(gathered_at, "grid", scatter_dimension=1, tiled=True)
    return summed.transpose(0, 2, 1).reshape(owned_blocks * TB, summed.shape[1])


def solution(mesh):
    placed = (
        P(("grid", "basis"), None, None),
        P(("grid", "basis"), None),
        P(("grid", "basis"), None, None),
        P(("grid", "basis"), None),
        P("basis", "grid"),
        P("basis", None),
        P(),
        P(),
        P(),
    )
    return jax.shard_map(
        body, mesh=mesh, in_specs=placed, out_specs=P("basis", "grid"), check_vma=False
    )
```

profile of v0, /device:TPU:27, one launch (start us, length us, event | category | flops | bytes accessed | tf_op | source)
XLA Modules:
  0.0 570.7 jit_solution(1581730656510795197)
XLA Ops:
  6.5 0.8 copy.210
  7.9 0.7 scatter_custom_fusion
  8.6 0.2 convert_reduce_fusion
  8.8 0.6 scatter_custom_fusion.1
  9.4 0.7 all_to_all.17
  10.1 4.5 all-to-all-start
  14.6 3.4 copy.252
  18.0 3.6 copy.272
  21.6 0.6 reshape.367
  22.2 4.2 all-to-all-start.1
  26.6 3.1 all-to-all-done.1
  29.8 12.3 %gather_fusion.5 = bf16[256,128,128]{2,1,0:T(8,128)(2,1)} fusion(bf16[4,32,128,128]{3,2,1,0:T(8,128)(2,1)} %bitcast.154, s32[256]{0:T(256)S(1)} %reshape.425), kind=kCustom, calls=%fused_computation.5 | custom fusion | bytes 16779264 | tf_op jit(solution)/shard_map/gather | solution.py:121
  42.1 6.5 %all-to-all-start.2 = ((bf16[8,4,8,128,128]{4,3,2,1,0:T(8,128)(2,1)}), bf16[8,4,8,128,128]{4,3,2,1,0:T(8,128)(2,1)}, u32[]{:S(2)}, u32[]{:S(2)}) async-start(bf16[8,4,8,128,128]{4,3,2,1,0:T(8,128)(2,1)} %bitcast.155), calls=%async_computation.2 | async-start | bytes 16777216 | tf_op jit(solution)/shard_map/all_to_all | solution.py:122
  49.1 6.9 %reshape.371 = bf16[16,256,4,128]{3,2,1,0:T(4,128)(2,1)} reshape(bf16[16,256,512]{2,1,0:T(8,128)(2,1)} %param.11) | data formatting | bytes 8388608 | tf_op jit(solution)/shard_map/reshape | solution.py:128
  56.1 0.6 copy.219
  56.8 2.8 gather_fusion.4
  59.6 0.2 copy.220
  59.8 1.2 multiply_reduce_fusion.1
  61.1 0.6 fusion.18
  61.7 0.6 copy.251
  62.3 0.6 copy.228
  63.8 4.0 multiply_convert_fusion
  67.8 6.9 %reshape.377 = bf16[16,256,4,128]{3,2,1,0:T(4,128)(2,1)} reshape(bf16[16,256,512]{2,1,0:T(8,128)(2,1)} %multiply_convert_fusion) | data formatting | bytes 8388608 | tf_op jit(solution)/shard_map/reshape | solution.py:148
  74.7 7.9 %convolution_convert_fusion = bf16[16,256,128,8]{2,3,1,0:T(8,128)(2,1)} fusion(bf16[16,256,4,128]{3,2,1,0:T(4,128)(2,1)} %reshape.377, s32[16,4]{1,0:T(8,128)S(1)} %copy.242), kind=kOutput, calls=%fused_computation.41 | convolution fusion | flops 37749248 | bytes 12583168 | tf_op jit(solution)/shard_map/ktc,kpti->kpci/dot_general | solution.py:145
  82.6 58.5 %all-to-all-done.2 = bf16[8,4,8,128,128]{4,3,2,1,0:T(8,128)(2,1)} async-done(((bf16[8,4,8,128,128]{4,3,2,1,0:T(8,128)(2,1)}), bf16[8,4,8,128,128]{4,3,2,1,0:T(8,128)(2,1)}, u32[]{:S(2)}, u32[]{:S(2)}) %all-to-all-start.2) | async-done | bytes 8388640 | tf_op jit(solution)/shard_map/all_to_all | solution.py:122
  141.1 5.5 gather_fusion.6
  146.7 11.6 %gather_fusion.7 = bf16[256,128,128]{2,1,0:T(8,128)(2,1)} fusion(bf16[8,8,128,128]{3,2,1,0:T(8,128)(2,1)} %gather_fusion.6, s32[256]{0:T(256)S(1)} %reshape.439), kind=kCustom, calls=%fused_computation.7 | custom fusion | bytes 16779264 | tf_op jit(solution)/shard_map/gather | solution.py:124
  158.3 8.9 %bitcast_convert_fusion = bf16[16,4,128,256]{3,2,1,0:T(8,128)(2,1)} fusion(bf16[16,4,4,128,128]{4,3,2,1,0:T(8,128)(2,1)} %bitcast.160, bf16[16,256,4,128,1]{3,2,1,0,4:T(4,128)(2,1)} %bitcast.164), kind=kOutput, calls=%fused_computation.39 | convolution fusion | flops 2149580800 | bytes 16777216 | tf_op jit(solution)/shard_map/ktuij,kpuj->kpti/dot_general | solution.py:125
  167.2 34.6 %while.10 = (s32[]{:T(128)}, bf16[4,4,256,4,128]{2,4,3,1,0:T(8,128)(2,1)}, s32[4,4,4]{2,1,0:T(4,128)S(1)}, bf16[8,128,8,128]{3,1,2,0:T(8,128)(2,1)S(1)}, bf16[4,...) while((s32[]{:T(128)}, ...), condition=%wide.region_10.11_spmd, body=%wide.region_7.10_spmd.sunk | while | flops 540742336 | bytes 10920305 | solution.py:76
  167.3 0.6 gather_fusion
  168.2 0.7 gather_fusion.1
  169.0 0.1 bitcast_divide_fusion.2
  169.4 2.1 gather_fusion.2
  171.5 3.2 fusion.56
  174.7 1.2 bitcast_dynamic-update-slice_fusion.2
  176.0 0.6 gather_fusion
  176.9 0.7 gather_fusion.1
  178.1 2.1 gather_fusion.2
  180.2 3.2 fusion.56
  183.4 1.1 bitcast_dynamic-update-slice_fusion.2
  184.6 0.6 gather_fusion
  185.5 0.7 gather_fusion.1
  186.4 0.1 bitcast_divide_fusion.2
  186.7 2.1 gather_fusion.2
  188.9 3.2 fusion.56
  192.1 1.1 bitcast_dynamic-update-slice_fusion.2
  193.2 0.6 gather_fusion
  194.2 0.7 gather_fusion.1
  195.3 2.1 gather_fusion.2
  197.5 3.2 fusion.56
  200.7 1.1 bitcast_dynamic-update-slice_fusion.2
  201.8 7.4 %copy.234 = bf16[16,256,4,128]{3,2,1,0:T(4,128)(2,1)} copy(bf16[16,256,4,128]{1,3,2,0:T(8,128)(2,1)} %bitcast.34) | data formatting | bytes 8388608 | tf_op jit(solution)/shard_map/reshape | solution.py:77
  209.2 7.9 %convolution_convert_fusion.1 = bf16[16,256,128,8]{2,3,1,0:T(8,128)(2,1)} fusion(bf16[16,256,4,128]{3,2,1,0:T(4,128)(2,1)} %copy.234, s32[16,4]{1,0:T(8,128)S(1)} %bitcast.170), kind=kOutput, calls=%fused_computation.42 | convolution fusion | flops 37749248 | bytes 12583168 | tf_op jit(solution)/shard_map/ktc,kpti->kpci/dot_general | solution.py:155
  217.1 15.3 %fusion.7 = f32[1024,1024]{1,0:T(8,128)} fusion(bf16[512,8,8,128]{3,2,1,0:T(8,128)(2,1)} %bitcast.159, bf16[512,8,8,128]{3,2,1,0:T(8,128)(2,1)} %bitcast.161), kind=kOutput, calls=%fused_computation.34 | convolution fusion | flops 8589934592 | bytes 20971520 | tf_op jit(solution)/shard_map/ka,kb->ab/dot_general | solution.py:160
  232.4 76.2 %reduce-scatter.3.cloned.1.call-done = f32[256,1024]{1,0:T(8,128)} async-done(((f32[1024,1024]{1,0:T(8,128)}), f32[256,1024]{1,0:T(8,128)}) %reduce-scatter.3.cloned.1.call-update) | async-done | bytes 1048592 | tf_op jit(solution)/shard_map/reduce_scatter | solution.py:159
  308.6 1.3 bitcast_bitcast_fusion
  309.9 2.4 broadcast_in_dim.61
  312.4 2.9 scatter_fusion
  315.2 5.3 all-to-all-start.3
  320.7 0.7 gather_fusion.3
  321.9 46.3 %all-to-all-done.3 = f32[8,4,256,128]{3,2,1,0:T(8,128)} async-done(((f32[8,4,256,128]{3,2,1,0:T(8,128)}), f32[8,4,256,128]{3,2,1,0:T(8,128)}, u32[]{:S(2)}, u32[]{:S(2)}) %all-to-all-start.3) | async-done | bytes 4194336 | tf_op jit(solution)/shard_map/all_to_all | solution.py:170
  368.2 48.3 %scatter_custom_fusion.3 = f32[16384,128]{1,0:T(8,128)} fusion(s32[8192]{0:T(1024)S(1)} %bitcast.173, f32[8192,128]{1,0:T(8,128)} %bitcast.43, f32[]{:T(128)} %constant.58.clone.1), kind=kCustom, calls=%fused_computation.46 | custom fusion | flops 1048576 | bytes 8389120
  416.5 144.5 %reduce-scatter.5.cloned.1.call-done = f32[4,1024,128]{2,1,0:T(8,128)} async-done(((f32[4,4096,128]{2,1,0:T(8,128)}), f32[4,1024,128]{2,1,0:T(8,128)}) %reduce-scatter.5.cloned.1.call-update) | async-done | bytes 2097168 | tf_op jit(solution)/shard_map/reduce_scatter | solution.py:184
  560.9 2.9 copy.236
  (120 shorter events, 5.8 us)
Async XLA Ops:
  10.1 11.5 %all-to-all-start = ((s32[8,1,4]{2,1,0:T(1,128)}), s32[8,1,4]{2,1,0:T(1,128)S(1)}, u32[]{:S(2)}, u32[]{:S(2)}) async-start(s32[8,1,4]{2,1,0:T(1,128)} %bitcast.14), calls=%async_computation | async-start | bytes 8192 | tf_op jit(solution)/shard_map/all_to_all | solution.py:117
  22.2 7.5 %all-to-all-start.1 = ((s32[8,4,8]{2,1,0:T(4,128)}), s32[8,4,8]{2,1,0:T(4,128)S(1)}, u32[]{:S(2)}, u32[]{:S(2)}) async-start(s32[8,4,8]{2,1,0:T(4,128)} %reshape.367), calls=%async_computation.1 | async-start | bytes 32768 | tf_op jit(solution)/shard_map/all_to_all | solution.py:110
  42.1 6.5 %copy-start.4 = (s32[16,4]{0,1:T(4,128)S(1)}, s32[16,4]{0,1:T(4,128)}, u32[]{:S(2)}) copy-start(s32[16,4]{0,1:T(4,128)} %param.14) | copy-start | bytes 772
  42.1 99.1 %all-to-all-start.2 = ((bf16[8,4,8,128,128]{4,3,2,1,0:T(8,128)(2,1)}), bf16[8,4,8,128,128]{4,3,2,1,0:T(8,128)(2,1)}, u32[]{:S(2)}, u32[]{:S(2)}) async-start(bf16[8,4,8,128,128]{4,3,2,1,0:T(8,128)(2,1)} %bitcast.155), calls=%async_computation.2 | async-start | bytes 16777216 | tf_op jit(solution)/shard_map/all_to_all | solution.py:122
  48.6 260.1 %reduce-scatter.3.cloned.1.call-start = ((), (), s32[]{:S(2)}) async-start(), calls=%async_computation.6 | async-start | bytes 5242880 | tf_op jit(solution)/shard_map/reduce_scatter | solution.py:159
  49.1 7.0 %copy-start.1 = (f32[3,4096]{1,0:T(4,128)S(1)}, f32[3,4096]{1,0:T(4,128)}, u32[]{:S(2)}) copy-start(f32[3,4096]{1,0:T(4,128)} %param.17) | copy-start | bytes 147460
  61.7 1.2 copy-start.2
  61.7 1.3 copy-start.5
  61.7 2.0 copy-start.3
  158.3 8.9 %copy-start = (f32[32]{0:T(128)S(1)}, f32[32]{0:T(128)}, u32[]{:S(2)}) copy-start(f32[32]{0:T(128)} %param.19) | copy-start | bytes 388
  315.2 6.4 %copy-start.7 = (s32[2]{0:T(128)S(1)}, s32[2]{0:T(128)}, u32[]{:S(2)}) copy-start(s32[2]{0:T(128)} %constant.142) | copy-start | bytes 28
  315.2 6.5 %copy-start.6 = (s32[2]{0:T(128)S(1)}, s32[2]{0:T(128)}, u32[]{:S(2)}) copy-start(s32[2]{0:T(128)} %constant.145) | copy-start | bytes 28
  315.2 52.9 %all-to-all-start.3 = ((f32[8,4,256,128]{3,2,1,0:T(8,128)}), f32[8,4,256,128]{3,2,1,0:T(8,128)}, u32[]{:S(2)}, u32[]{:S(2)}) async-start(f32[8,4,256,128]{3,2,1,0:T(8,128)} %bitcast.157), calls=%async_computation.4 | async-start | bytes 8388608 | tf_op jit(solution)/shard_map/all_to_all | solution.py:170
  320.5 240.4 %reduce-scatter.5.cloned.1.call-start = ((), (), s32[]{:S(2)}) async-start(), calls=%async_computation.7 | async-start | bytes 10485760 | tf_op jit(solution)/shard_map/reduce_scatter | solution.py:184
Sparse Core Ops, SparseCore 0:
  232.5 76.0 reduce-scatter.2
  416.6 144.2 reduce-scatter.4
where the time goes:
time: 574 us; the launch traced here: 571 us
  waiting for transfers between devices  329 us (57%)
  local copies, waits for them, and re-layouts  96.7 us (17%)
  other arithmetic  57.5 us (10%)
  matrix products  52.7 us (9%)
  starting transfers between devices  20.5 us (4%)
  between operations  14.3 us (2%)
    reduce_scatter x1, waiting for transfers between devices, body(): lax.psum_scatter(gathered_at, 'grid', scatter_dimension=1, tiled=True)  144 us
    reduce_scatter x1, waiting for transfers between devices, body(): lax.psum_scatter(jnp.einsum('ka,kb->ab', spread_cols, spread_rows, prefer...  76.2 us
    all_to_all x1, waiting for transfers between devices, body(): lax.all_to_all(tile_rows, 'basis', split_axis=0, concat_axis=0, tiled=True)  58.5 us
    unnamed x5, other arithmetic  49.1 us
    all_to_all x1, waiting for transfers between devices, body(): lax.all_to_all(outgoing.reshape(basis_size, per_owner, seg_width, TB), 'b...  46.3 us
    dot_general x1, matrix products, body(): jnp.einsum('ka,kb->ab', spread_cols, spread_rows, preferred_element_type=...  15.3 us
    dot_general x4, matrix products, one_group(): jnp.einsum('kpuj,ktuij->kptui', mapped_part, coupled, preferred_element_t...  12.8 us
    gather x1, local copies, waits for them, and re-layouts, body(): tile_rows = density_tiles[safe_rows[:, :, None], columns_in]  12.3 us
  transfers between devices with their start and end apart: 6, of which 5 were waited for; matrix products, arithmetic and copies ran while one was open for 7% of the time, Pallas kernels for 0%

commit v1 on v0

v1 whole, which is shorter than its diff:
```python
import functools
import math

import jax
import jax.numpy as jnp
import numpy as np
from jax import lax
from jax.experimental import pallas as pl
from jax.experimental.pallas import tpu as pltpu
from jax.sharding import PartitionSpec as P

TB = 128
CL = 8


def boys_table(points_f, blocks, block_centers, block_exponents):
    centre = block_centers[:, blocks]
    middle = 0.5 * (centre[:, :, :, None] + centre[:, :, None, :])
    exponents = block_exponents[blocks]
    rate_pair = 0.5 * (exponents[:, :, None] + exponents[:, None, :])
    offset = points_f.transpose(1, 0, 2)[:, :, None, None, :] - middle[:, :, :, :, None]
    distance = jnp.sum(offset * offset, axis=0)
    tau_value = rate_pair[:, :, :, None] * distance + 0.05
    root_value = jnp.sqrt(tau_value)
    return 0.5 * math.sqrt(math.pi) * lax.erf(root_value) / root_value


def first_block_of(block_lists, block_count):
    present = jnp.any(
        block_lists.reshape(-1)[:, None] == jnp.arange(block_count, dtype=jnp.int32)[None, :],
        axis=0,
    )
    begins = present & jnp.logical_not(jnp.roll(present, 1))
    return jnp.sum(jnp.where(begins, jnp.arange(block_count, dtype=jnp.int32), 0))


def block_with_residue(first, residue, block_count):
    return (first + (residue - first) % CL) % block_count


def region_coupling(members, centers):
    functions = (members[:, None] * TB + jnp.arange(TB, dtype=jnp.int32)[None, :]).reshape(CL * TB)
    where_at = centers[:, functions].reshape(3, CL, TB)
    spread = where_at[:, :, None, :, None] - where_at[:, None, :, None, :]
    distance = jnp.sum(spread * spread, axis=0)
    sharpness = float(centers.shape[1]) ** (2.0 / 3.0)
    return jnp.exp(-sharpness * distance).astype(jnp.bfloat16)


def pack_kernel(column_ref, dens_ref, out_ref):
    out_ref[0, :, 0] = dens_ref[...].reshape(out_ref.shape[1], TB, TB)


def pack_density(columns, density, owned_blocks):
    targets, per = columns.shape
    return pl.pallas_call(
        pack_kernel,
        grid_spec=pltpu.PrefetchScalarGridSpec(
            num_scalar_prefetch=1,
            grid=(targets, per),
            in_specs=[pl.BlockSpec((owned_blocks * TB, TB), lambda t, c, col: (0, col[t, c]))],
            out_specs=pl.BlockSpec(
                (1, owned_blocks, 1, TB, TB), lambda t, c, col: (t, 0, c, 0, 0)
            ),
        ),
        out_shape=jax.ShapeDtypeStruct((targets, owned_blocks, per, TB, TB), jnp.bfloat16),
        name="pack_density",
    )(columns, density)


def batch_kernel(
    per, place_ref, count_ref, values_ref, weighted_ref, boys_ref, dens_ref, coup_ref, out_ref, acc
):
    n = pl.program_id(0)
    lists = place_ref.shape[1]

    @pl.when(n == 0)
    def _():
        acc[...] = jnp.zeros_like(acc)

    @pl.when(n < count_ref[0])
    def _():
        at = [place_ref[n, t] for t in range(lists)]
        dens = jnp.concatenate(
            [
                jnp.concatenate([dens_ref[c // per, r, c % per] for c in at], axis=1)
                for r in at
            ],
            axis=0,
        )
        mapped = lax.dot_general(
            dens, values_ref[0], (((1,), (1,)), ((), ())), preferred_element_type=jnp.float32
        ).astype(jnp.bfloat16)
        total = None
        for u in range(lists):
            coup = jnp.concatenate([coup_ref[r, at[u]] for r in at], axis=0)
            part = jnp.dot(
                coup, mapped[u * TB : (u + 1) * TB], preferred_element_type=jnp.float32
            )
            part = jnp.concatenate(
                [
                    part[t * TB : (t + 1) * TB]
                    * boys_ref[0, t * lists + u : t * lists + u + 1, :]
                    for t in range(lists)
                ],
                axis=0,
            )
            total = part if total is None else total + part
        tile = jnp.dot(
            total.astype(jnp.bfloat16), weighted_ref[0], preferred_element_type=jnp.float32
        )
        for c in range(lists):
            for r in range(lists):
                acc[at[c], at[r]] += tile[c * TB : (c + 1) * TB, r * TB : (r + 1) * TB]

    @pl.when(n == pl.num_programs(0) - 1)
    def _():
        def put(index, carry):
            c = index // CL
            r = index % CL
            out_ref[c // per, r, c % per] = acc[c, r].T.astype(out_ref.dtype)
            return carry

        lax.fori_loop(0, CL * CL, put, 0)


def region_exchange(places, count, values, weighted, boys, dens, coup, grid_size):
    batches, points, listed = values.shape
    per = CL // grid_size
    lists = places.shape[1]
    whole = lambda *shape: pl.BlockSpec(shape, lambda n, *_: (0,) * len(shape))
    return pl.pallas_call(
        functools.partial(batch_kernel, per),
        grid_spec=pltpu.PrefetchScalarGridSpec(
            num_scalar_prefetch=2,
            grid=(batches,),
            in_specs=[
                pl.BlockSpec((1, points, listed), lambda n, *_: (n, 0, 0)),
                pl.BlockSpec((1, points, listed), lambda n, *_: (n, 0, 0)),
                pl.BlockSpec((1, lists * lists, points), lambda n, *_: (n, 0, 0)),
                whole(grid_size, CL, per, TB, TB),
                whole(CL, CL, TB, TB),
            ],
            out_specs=whole(grid_size, CL, per, TB, TB),
            scratch_shapes=[pltpu.VMEM((CL, CL, TB, TB), jnp.float32)],
        ),
        out_shape=jax.ShapeDtypeStruct((grid_size, CL, per, TB, TB), jnp.bfloat16),
        compiler_params=pltpu.CompilerParams(vmem_limit_bytes=48 * 1024 * 1024),
        name="region_exchange",
    )(places, count, values, weighted, boys, dens, coup)


def body(
    basis_values,
    weights,
    points,
    block_lists,
    counts,
    density,
    centers,
    block_centers,
    block_exponents,
):
    basis_size = lax.axis_size("basis")
    grid_size = lax.axis_size("grid")
    me_basis = lax.axis_index("basis")
    me_grid = lax.axis_index("grid")
    block_count = block_exponents.shape[0]
    owned_blocks = block_count // basis_size
    turns = block_count // CL
    per = CL // grid_size
    batches, point_total = weights.shape
    lists = block_lists.shape[1]

    first = first_block_of(block_lists, block_count)
    firsts = lax.all_to_all(
        jnp.broadcast_to(first, (basis_size, 1)), "basis", split_axis=0, concat_axis=0, tiled=True
    )[:, 0]
    my_residues = me_grid * per + jnp.arange(per, dtype=jnp.int32)
    columns = block_with_residue(firsts[:, None], my_residues[None, :], block_count)

    packed = pack_density(columns, density, owned_blocks)
    tiles_in = lax.all_to_all(packed, "basis", split_axis=0, concat_axis=0, tiled=True)
    members = block_with_residue(first, jnp.arange(CL, dtype=jnp.int32), block_count)
    turn_of = members // CL
    chosen = (turn_of[None, :] == jnp.arange(turns, dtype=jnp.int32)[:, None])
    by_turn = tiles_in.reshape(turns, CL, per, TB, TB)
    mine = by_turn[0]
    for turn in range(1, turns):
        mine = jnp.where(chosen[turn][:, None, None, None], by_turn[turn], mine)
    dens = lax.all_to_all(
        jnp.broadcast_to(mine[None], (grid_size,) + mine.shape),
        "grid",
        split_axis=0,
        concat_axis=0,
        tiled=True,
    )

    coup = region_coupling(members, centers)
    boys = boys_table(
        points.astype(jnp.float32), block_lists, block_centers, block_exponents
    ).reshape(batches, lists * lists, point_total)
    live_count = counts[0, 0]
    is_live = jnp.arange(batches, dtype=jnp.int32) < live_count
    scaled = jnp.where(is_live[:, None], weights, 0.0) / point_total
    weighted = (basis_values * scaled[:, :, None]).astype(jnp.bfloat16)

    partial_sums = region_exchange(
        block_lists % CL, counts.reshape(1), basis_values, weighted, boys, dens, coup, grid_size
    )
    shares = lax.all_to_all(partial_sums, "grid", split_axis=0, concat_axis=0, tiled=True)
    segment = jnp.sum(shares.astype(jnp.float32), axis=0)

    outgoing = jnp.broadcast_to(segment[None], (turns,) + segment.shape).reshape(
        basis_size, owned_blocks, per, TB, TB
    )
    incoming = lax.all_to_all(outgoing, "basis", split_axis=0, concat_axis=0, tiled=True)
    my_blocks = me_basis * owned_blocks + jnp.arange(owned_blocks, dtype=jnp.int32)
    inside = (my_blocks[None, :] - firsts[:, None]) % block_count < CL
    takes = (
        inside[:, None, :, None]
        & (columns[:, None, None, :] // CL == jnp.arange(turns, dtype=jnp.int32)[None, :, None, None])
    )
    held = jnp.sum(
        jnp.where(takes[..., None, None], incoming[:, None], 0.0), axis=0
    )

    per_owner = block_count // grid_size
    if per_owner == CL:
        got = lax.all_to_all(held, "grid", split_axis=0, concat_axis=0, tiled=True)
        return got.transpose(1, 3, 0, 2, 4).reshape(owned_blocks * TB, per_owner * TB)
    held_blocks = np.array(
        [[q * CL + j * per + c for q in range(turns) for c in range(per)] for j in range(grid_size)]
    )
    room = max(
        int(np.sum(held_blocks[j] // per_owner == k))
        for j in range(grid_size)
        for k in range(grid_size)
    )
    send = np.zeros((grid_size, grid_size, room), np.int32)
    source = np.zeros((grid_size, per_owner), np.int32)
    for j in range(grid_size):
        filled = [0] * grid_size
        for at, block in enumerate(held_blocks[j]):
            k = int(block) // per_owner
            send[j, k, filled[k]] = at
            source[k, int(block) % per_owner] = j * room + filled[k]
            filled[k] += 1
    flat = held.transpose(0, 2, 1, 3, 4).reshape(turns * per, owned_blocks, TB, TB)
    going = flat[jnp.asarray(send)[me_grid].reshape(-1)].reshape(
        grid_size, room, owned_blocks, TB, TB
    )
    got = lax.all_to_all(going, "grid", split_axis=0, concat_axis=0, tiled=True)
    picked = got.reshape(grid_size * room, owned_blocks, TB, TB)[jnp.asarray(source)[me_grid]]
    return picked.transpose(1, 2, 0, 3).reshape(owned_blocks * TB, per_owner * TB)


def solution(mesh):
    placed = (
        P(("grid", "basis"), None, None),
        P(("grid", "basis"), None),
        P(("grid", "basis"), None, None),
        P(("grid", "basis"), None),
        P("basis", "grid"),
        P("basis", None),
        P(),
        P(),
        P(),
    )
    return jax.shard_map(
        body, mesh=mesh, in_specs=placed, out_specs=P("basis", "grid"), check_vma=False
    )
```

time: 574 us -> 300 us (0.52)
  waiting for transfers between devices: 329 us -> 103 us
  blocking collectives: 0 us -> 108 us
  local copies, waits for them, and re-layouts: 96.7 us -> 21.7 us
  matrix products: 52.7 us -> 0 us
  other arithmetic: 57.5 us -> 13.7 us
  Pallas kernels: 0 us -> 30.2 us
  between operations: 14.3 us -> 0.89 us
    reduce_scatter x2 -> x0, waiting for transfers between devices: 221 us -> none  [the longest x1 144 us: body(): lax.psum_scatter(gathered_at, 'grid', scatter_dimension=1, tiled=True)]
    all_to_all x0 -> x2, blocking collectives: none -> 108 us  [the longest x1 57.5 us: body(): lax.all_to_all(partial_sums, 'grid', split_axis=0, concat_axis=0, tiled=T...]
    dot_general x8 -> x0, matrix products: 52.7 us -> none  [the longest x1 15.3 us: body(): jnp.einsum('ka,kb->ab', spread_cols, spread_rows, preferred_element_type=...]
    unnamed x5 -> x0, other arithmetic: 49.1 us -> none
    gather x10 -> x1, local copies, waits for them, and re-layouts: 41.7 us -> 4.39 us  [region_coupling(): where_at = centers[:, functions].reshape(3, CL, TB)]
    pallas_call x0 -> x2, Pallas kernels: none -> 30.2 us  [the longest x1 19.9 us: region_exchange(): pl.pallas_call(functools.partial(batch_kernel, per), grid_spec=pltpu.Pref...]
    reshape x6 -> x1, local copies, waits for them, and re-layouts: 25.5 us -> 2.68 us  [body(): got.transpose(1, 3, 0, 2, 4).reshape(owned_blocks * TB, per_owner * TB)]
  transfers between devices with their start and end apart: 6 -> 4, of which waited for: 5 -> 4; matrix products, arithmetic and copies ran while one was open for 7% -> 5% of each run, Pallas kernels for 0% -> 0%
where the time goes in v1:
time: 300 us; the launch traced here: 297 us
  blocking collectives  108 us (36%)
  waiting for transfers between devices  103 us (34%)
  Pallas kernels  30.2 us (10%)
  local copies, waits for them, and re-layouts  21.7 us (7%)
  starting transfers between devices  19 us (6%)
  other arithmetic  13.7 us (5%)
    all_to_all x1, blocking collectives, body(): lax.all_to_all(partial_sums, 'grid', split_axis=0, concat_axis=0, tiled=T...  57.5 us
    all_to_all x1, blocking collectives, body(): got = lax.all_to_all(held, 'grid', split_axis=0, concat_axis=0, tiled=True)  50.6 us
    all_to_all x1, waiting for transfers between devices, body(): lax.all_to_all(outgoing, 'basis', split_axis=0, concat_axis=0, tiled=True)  46.9 us
    all_to_all x1, waiting for transfers between devices, body(): lax.all_to_all(jnp.broadcast_to(mine[None], (grid_size,) + mine.shape), '...  29.1 us
    all_to_all x1, waiting for transfers between devices, body(): lax.all_to_all(packed, 'basis', split_axis=0, concat_axis=0, tiled=True)  24.4 us
    pallas_call x1, Pallas kernels, region_exchange(): pl.pallas_call(functools.partial(batch_kernel, per), grid_spec=pltpu.Pref...  19.9 us
    pallas_call x1, Pallas kernels, pack_density(): pl.pallas_call(pack_kernel, grid_spec=pltpu.PrefetchScalarGridSpec(num_sc...  10.2 us
  transfers between devices with their start and end apart: 4, of which 4 were waited for; matrix products, arithmetic and copies ran while one was open for 5% of the time, Pallas kernels for 0%

profile of v1, /device:TPU:27, one launch (start us, length us, event | category | flops | bytes accessed | tf_op | source)
XLA Modules:
  0.0 296.7 jit_solution(1054141613786263313)
XLA Ops:
  0.0 0.0 copy-start
  0.0 0.8 copy.68
  0.8 0.1 eq.56
  0.9 0.1 fusion.4
  1.0 0.6 slice.33
  1.6 1.3 fusion.18
  2.9 1.2 broadcast_in_dim.102
  4.1 4.5 %all-to-all-start = ((s32[8,1,1]{2,1,0:T(1,128)}), s32[8,1,1]{2,1,0:T(1,128)S(1)}, u32[]{:S(2)}, u32[]{:S(2)}) async-start(s32[8,1,1]{2,1,0:T(1,128)} %broadcast_in_dim.102), calls=%async_computation | async-start | bytes 8192 | tf_op jit(solution)/shard_map/all_to_all | solution.py:176
  8.6 2.8 all-to-all-done
  11.5 0.2 reduce
  11.7 0.7 add_select_fusion.1
  12.4 10.2 %pack_density.1 = bf16[8,4,2,128,128]{4,3,2,1,0:T(8,128)(2,1)} custom-call(s32[8,2]{1,0:T(8,128)} %get-tuple-element.12.column_ref, bf16[512,4096]{1,0:T(8,128)(2,1)} %dens_ref.1), custom_call_target="tpu_custom_call" | custom-call | tf_op jit(solution)/shard_map/pack_density/pallas_call | solution.py:56
  22.6 5.3 %all-to-all-start.1 = ((bf16[8,4,2,128,128]{4,3,2,1,0:T(8,128)(2,1)}), bf16[8,4,2,128,128]{4,3,2,1,0:T(8,128)(2,1)S(1)}, u32[]{:S(2)}, u32[]{:S(2)}) async-start(bf16[8,4,2,128,128]{4,3,2,1,0:T(8,128)(2,1)} %pack_density.1), calls=%async_computation.1 | async-start | bytes 4194304 | tf_op jit(solution)/shard_map/all_to_all | solution.py:183
  27.9 0.6 and_select_fusion
  28.5 0.1 iota_add_fusion
  28.6 24.4 %all-to-all-done.1 = bf16[8,4,2,128,128]{4,3,2,1,0:T(8,128)(2,1)S(1)} async-done(((bf16[8,4,2,128,128]{4,3,2,1,0:T(8,128)(2,1)}), bf16[8,4,2,128,128]{4,3,2,1,0:T(8,128)(2,1)S(1)}, u32[]{:S(2)}, u32[]{:S(2)}) %all-to-all-start.1) | async-done | bytes 2097184 | tf_op jit(solution)/shard_map/all_to_all | solution.py:183
  53.0 0.2 fusion.19
  53.2 0.0 copy-start.2
  53.2 0.2 fusion.1
  53.4 1.9 broadcast_in_dim.113
  55.3 0.0 copy-start.5
  55.3 4.7 %all-to-all-start.2 = ((bf16[4,8,2,128,128]{4,3,2,1,0:T(8,128)(2,1)}), bf16[4,8,2,128,128]{4,3,2,1,0:T(8,128)(2,1)S(1)}, u32[]{:S(2)}, u32[]{:S(2)}) async-start(bf16[4,8,2,128,128]{4,3,2,1,0:T(8,128)(2,1)} %broadcast_in_dim.113), calls=%async_computation.2 | async-start | bytes 4194304 | tf_op jit(solution)/shard_map/all_to_all | solution.py:191
  60.0 0.0 copy-done.2
  60.0 2.0 copy.81
  62.0 4.4 %gather_fusion.2 = f32[1024,3]{1,0:T(8,128)S(1)} fusion(f32[3,4096]{0,1:T(8,128)} %copy.81, s32[1024]{0:T(1024)S(1)} %broadcast_clamp_fusion), kind=kCustom, calls=%fused_computation.2 | custom fusion | bytes 28672 | tf_op jit(solution)/shard_map/gather | solution.py:43
  66.4 0.2 copy.82
  66.6 0.1 reshape.325
  66.7 0.0 copy-done.5
  66.7 0.1 copy.77
  66.8 0.6 gather_fusion.1
  67.4 0.1 copy.78
  67.5 0.0 copy-done
  67.5 0.0 copy-start.3
  67.5 0.0 copy-start.4
  67.5 0.8 gather_fusion
  68.3 0.1 reshape.324
  68.4 0.1 copy.74
  68.5 0.1 copy.76
  69.2 0.0 copy-done.3
  69.3 0.2 multiply_reduce_fusion.1
  69.4 0.0 copy-done.4
  69.4 0.1 select_multiply_fusion
  69.5 0.2 multiply_divide_fusion.boys_ref
  69.8 1.3 multiply_reduce_fusion
  71.0 0.0 copy-start.1
  71.0 1.9 exponential_convert_fusion.coup_ref
  73.0 1.0 copy-done.1
  74.0 2.4 multiply_convert_fusion.weighted_ref
  76.4 29.1 %all-to-all-done.2.dens_ref = bf16[4,8,2,128,128]{4,3,2,1,0:T(8,128)(2,1)S(1)} async-done(((bf16[4,8,2,128,128]{4,3,2,1,0:T(8,128)(2,1)}), bf16[4,8,2,128,128]{4,3,2,1,0:T(8,128)(2,1)S(1)}, u32[]{:S(2)}, u32[]{:S(2)}) %all-to-all-start.2) | async-done | bytes 2097184 | tf_op jit(solution)/shard_map/all_to_all | solution.py:191
  105.5 19.9 %region_exchange.1 = bf16[4,8,2,128,128]{4,3,2,1,0:T(8,128)(2,1)S(1)} custom-call(s32[16,4]{1,0:T(8,128)S(1)} %get-tuple-element.10.place_ref, s32[1]{0:T(128)} %bitcast.35.count_ref, bf16[16,256,512]{2,1,0:T(8,128)(2,1)} %values_ref.1, bf16[16,256,512]{2,1,0:T(8,128)(2,1)} %multiply_convert_fusion.weighted_ref, ...), custom_call_target="tpu_custom_call" | custom-call | tf_op jit(solution)/shard_map/region_exchange/pallas_call | solution.py:132
  125.4 57.5 %all_to_all.31 = bf16[4,8,2,128,128]{4,3,2,1,0:T(8,128)(2,1)S(1)} all-to-all(bf16[4,8,2,128,128]{4,3,2,1,0:T(8,128)(2,1)S(1)} %region_exchange.1), channel_id=1, replica_groups=mesh['grid'=4,'basis'=8] {'grid'}, dimensions={0} | all-to-all | bytes 4194304 | tf_op jit(solution)/shard_map/all_to_all | solution.py:211
  182.9 0.4 convert_reduce_fusion
  183.3 2.5 broadcast_in_dim.114
  185.8 4.5 %all-to-all-start.4 = ((f32[8,4,2,128,128]{4,3,2,1,0:T(8,128)}), f32[8,4,2,128,128]{4,3,2,1,0:T(8,128)}, u32[]{:S(2)}, u32[]{:S(2)}) async-start(f32[8,4,2,128,128]{4,3,2,1,0:T(8,128)} %bitcast.37), calls=%async_computation.4 | async-start | bytes 8388608 | tf_op jit(solution)/shard_map/all_to_all | solution.py:217
  190.3 0.1 fusion.6
  190.4 0.1 broadcast_and_fusion
  190.5 46.9 %all-to-all-done.4 = f32[8,4,2,128,128]{4,3,2,1,0:T(8,128)} async-done(((f32[8,4,2,128,128]{4,3,2,1,0:T(8,128)}), f32[8,4,2,128,128]{4,3,2,1,0:T(8,128)}, u32[]{:S(2)}, u32[]{:S(2)}) %all-to-all-start.4) | async-done | bytes 4194336 | tf_op jit(solution)/shard_map/all_to_all | solution.py:217
  237.5 3.7 %select_reduce_fusion = f32[4,4,2,128,128]{4,3,2,1,0:T(8,128)S(1)} fusion(f32[8,4,2,128,128]{4,3,2,1,0:T(8,128)} %all-to-all-done.4, pred[8,4,4,2]{3,2,1,0:T(4,128)(4,1)S(1)} %broadcast_and_fusion), kind=kLoop, calls=%fused_computation.3 | loop fusion | flops 7864320 | bytes 6291712 | tf_op jit(solution)/shard_map/reduce_sum | solution.py:224
  241.1 1.6 copy.84
  242.8 50.6 %all_to_all.32 = f32[4,4,2,128,128]{4,2,3,1,0:T(2,128)S(1)} all-to-all(f32[4,4,2,128,128]{4,2,3,1,0:T(2,128)S(1)} %copy.84), channel_id=1, replica_groups=mesh['grid'=4,'basis'=8] {'grid'}, dimensions={0} | all-to-all | bytes 4194304 | tf_op jit(solution)/shard_map/all_to_all | solution.py:230
  293.3 0.7 copy.85
  294.1 2.7 reshape.322
  (13 shorter events, 0.1 us)
Async XLA Ops:
  0.0 67.5 %copy-start = (f32[32]{0:T(128)S(1)}, f32[32]{0:T(128)}, u32[]{:S(2)}) copy-start(f32[32]{0:T(128)} %param.17) | copy-start | bytes 388
  4.1 7.4 %all-to-all-start = ((s32[8,1,1]{2,1,0:T(1,128)}), s32[8,1,1]{2,1,0:T(1,128)S(1)}, u32[]{:S(2)}, u32[]{:S(2)}) async-start(s32[8,1,1]{2,1,0:T(1,128)} %broadcast_in_dim.102), calls=%async_computation | async-start | bytes 8192 | tf_op jit(solution)/shard_map/all_to_all | solution.py:176
  22.6 30.4 %all-to-all-start.1 = ((bf16[8,4,2,128,128]{4,3,2,1,0:T(8,128)(2,1)}), bf16[8,4,2,128,128]{4,3,2,1,0:T(8,128)(2,1)S(1)}, u32[]{:S(2)}, u32[]{:S(2)}) async-start(bf16[8,4,2,128,128]{4,3,2,1,0:T(8,128)(2,1)} %pack_density.1), calls=%async_computation.1 | async-start | bytes 4194304 | tf_op jit(solution)/shard_map/all_to_all | solution.py:183
  53.2 6.8 %copy-start.2 = (f32[3,4096]{1,0:T(4,128)S(1)}, f32[3,4096]{1,0:T(4,128)}, u32[]{:S(2)}) copy-start(f32[3,4096]{1,0:T(4,128)} %param.15) | copy-start | bytes 147460
  55.3 11.4 %copy-start.5 = (f32[3,32]{1,0:T(4,128)S(1)}, f32[3,32]{1,0:T(4,128)}, u32[]{:S(2)}) copy-start(f32[3,32]{1,0:T(4,128)} %param.16) | copy-start | bytes 1156
  55.3 50.1 %all-to-all-start.2 = ((bf16[4,8,2,128,128]{4,3,2,1,0:T(8,128)(2,1)}), bf16[4,8,2,128,128]{4,3,2,1,0:T(8,128)(2,1)S(1)}, u32[]{:S(2)}, u32[]{:S(2)}) async-start(bf16[4,8,2,128,128]{4,3,2,1,0:T(8,128)(2,1)} %broadcast_in_dim.113), calls=%async_computation.2 | async-start | bytes 4194304 | tf_op jit(solution)/shard_map/all_to_all | solution.py:191
  67.5 1.7 copy-start.3
  67.5 1.9 copy-start.4
  71.0 2.9 copy-start.1
  185.8 51.6 %all-to-all-start.4 = ((f32[8,4,2,128,128]{4,3,2,1,0:T(8,128)}), f32[8,4,2,128,128]{4,3,2,1,0:T(8,128)}, u32[]{:S(2)}, u32[]{:S(2)}) async-start(f32[8,4,2,128,128]{4,3,2,1,0:T(8,128)} %bitcast.37), calls=%async_computation.4 | async-start | bytes 8388608 | tf_op jit(solution)/shard_map/all_to_all | solution.py:217
